TPU v7x, 256 devices: a whole 4x4x8 slice. The times are simulated.
256 devices in a mesh: dp: 8 (over y_lo, x), lon: 32 (over y_hi, z, core).
Axes of the slice: x: 4, y: 4 (y_hi: 2, y_lo: 2; y = y_hi * 2 + y_lo), z: 8, core: 2. Of those that a mesh axis runs over, the one named last changes fastest.
Arguments:
- fields: bfloat16 [8, 64, 512, 384], P('dp', None, 'lon'), may hold values from -6 to 6
- cotangent: bfloat16 [8, 64, 512, 384], P('dp', None, 'lon'), may hold values from -6 to 6
- kernel_first: bfloat16 [3, 3, 64, 64], replicated, may hold values from -0.25 to 0.25
- kernel_second: bfloat16 [3, 3, 64, 64], replicated, may hold values from -0.25 to 0.25
- metric: float32 [384], replicated, may hold values from 0.5 to 3
Outputs:
- field_grad: bfloat16 [8, 64, 512, 384], P('dp', None, 'lon')
- grad_first: bfloat16 [3, 3, 64, 64], replicated
- grad_second: bfloat16 [3, 3, 64, 64], replicated
All inputs are finite; a program needn't handle non-finite values.
Results may differ from a plain program's by a relative error of at most 0.0063.
Values may be sent and summed in bfloat16 or wider, within the bound.
A program may use at most 64 MiB of HBM per device.

v0:
```python
import jax
import jax.numpy as jnp
from jax import lax
from jax.sharding import PartitionSpec as P

gelu_coef = 0.7978845608


def extended(shard, sides, width):
    for axis, dim in sides:
        count, length = (lax.axis_size(axis), shard.shape[dim])
        up = [(i, (i + 1) % count) for i in range(count)]
        down = [(j, i) for i, j in up]
        last = lax.slice_in_dim(shard, length - width, length, axis=dim)
        first = lax.slice_in_dim(shard, 0, width, axis=dim)
        before = lax.ppermute(last, axis, up)
        after = lax.ppermute(first, axis, down)
        shard = jnp.concatenate([before, shard, after], axis=dim)
    return shard


def gelu_value(u):
    inner = jnp.tanh(gelu_coef * (u + 0.044715 * u * u * u))
    return 0.5 * u * (1.0 + inner)


def gelu_slope(u):
    inner = jnp.tanh(gelu_coef * (u + 0.044715 * u * u * u))
    return 0.5 * (1.0 + inner) + 0.5 * u * (1.0 - inner * inner) * gelu_coef * (
        1.0 + 3.0 * 0.044715 * u * u
    )


def pad_rows(value):
    return jnp.pad(value, ((0, 0), (0, 0), (0, 0), (1, 1)))


def stencil_apply(padded, taps, metric):
    columns = padded.shape[2] - 2
    lat_rows = padded.shape[3] - 2
    total = None
    for p in range(3):
        summed = None
        for q in range(3):
            term = jnp.einsum(
                "oc,bcij->boij",
                taps[p, q],
                padded[:, :, p : p + columns, q : q + lat_rows],
                preferred_element_type=jnp.float32,
            )
            summed = term if summed is None else summed + term
        summed = summed if p == 1 else summed * metric[None, None, None, :]
        total = summed if total is None else total + summed
    return total


def stencil_adjoint(plain_pad, scaled_pad, taps):
    columns = plain_pad.shape[2] - 2
    lat_rows = plain_pad.shape[3] - 2
    total = None
    for p in range(3):
        source = plain_pad if p == 1 else scaled_pad
        for q in range(3):
            term = jnp.einsum(
                "oc,boij->bcij",
                taps[p, q],
                source[:, :, 2 - p : 2 - p + columns, 2 - q : 2 - q + lat_rows],
                preferred_element_type=jnp.float32,
            )
            total = term if total is None else total + term
    return total


def kernel_term(plain, scaled, padded):
    columns = plain.shape[2]
    lat_rows = plain.shape[3]
    terms = []
    for p in range(3):
        source = plain if p == 1 else scaled
        row_terms = []
        for q in range(3):
            row_terms.append(
                jnp.einsum(
                    "boij,bcij->oc",
                    source,
                    padded[:, :, p : p + columns, q : q + lat_rows],
                    preferred_element_type=jnp.float32,
                )
            )
        terms.append(jnp.stack(row_terms))
    return jnp.stack(terms)


def per_device(fields, cotangent, kernel_first, kernel_second, metric):
    metric_padded = jnp.pad(metric, (1, 1))[None, None, None, :]
    samples_here = fields.shape[0]
    stacked = jnp.concatenate((fields, cotangent), axis=0)
    both_pad = extended(stacked, (("lon", 2),), 1)
    input_pad = pad_rows(both_pad[:samples_here])
    upstream_pad = pad_rows(both_pad[samples_here:])
    before_gelu = stencil_apply(input_pad, kernel_first, metric)
    hidden = gelu_value(before_gelu).astype(jnp.bfloat16)
    hidden_pad = pad_rows(extended(hidden, (("lon", 2),), 1))
    scaled_pad = (metric_padded * upstream_pad.astype(jnp.float32)).astype(jnp.bfloat16)
    second = kernel_term(cotangent, scaled_pad[:, :, 1:-1, 1:-1], hidden_pad)
    hidden_grad = stencil_adjoint(upstream_pad, scaled_pad, kernel_second)
    delta = (hidden_grad * gelu_slope(before_gelu)).astype(jnp.bfloat16)
    delta_pad = pad_rows(extended(delta, (("lon", 2),), 1))
    delta_scaled = (metric_padded * delta_pad.astype(jnp.float32)).astype(jnp.bfloat16)
    field_grad = (
        cotangent.astype(jnp.float32) + stencil_adjoint(delta_pad, delta_scaled, kernel_first)
    ).astype(jnp.bfloat16)
    first = kernel_term(delta, delta_scaled[:, :, 1:-1, 1:-1], input_pad)
    first, second = lax.psum((first, second), ("dp", "lon"))
    counted = (
        float(fields.shape[0] * lax.axis_size("dp"))
        * float(fields.shape[2] * lax.axis_size("lon"))
        * float(fields.shape[3])
    )
    factor = jnp.float32(1.0 / counted**0.5)
    return (
        field_grad,
        (first * factor).astype(jnp.bfloat16),
        (second * factor).astype(jnp.bfloat16),
    )


def solution(mesh):
    placed = (P("dp", None, "lon", None), P("dp", None, "lon", None), P(), P(), P())
    return jax.shard_map(
        per_device,
        mesh=mesh,
        in_specs=placed,
        out_specs=(P("dp", None, "lon", None), P(), P()),
        check_vma=False,
    )
```

profile of v0, /device:TPU:1, one launch (start us, length us, event | category | flops | bytes accessed | tf_op | source)
XLA Modules:
  0.0 325.4 jit_solution(10439744815576890022)
XLA Ops:
  7.2 1.4 copy_dynamic-update-slice_fusion
  9.0 3.1 collective-permute-start
  13.7 2.4 collective-permute-done.1
  16.6 0.4 fusion.53
  17.0 0.4 fusion.56
  17.5 0.4 fusion.59
  17.9 0.4 fusion.62
  18.3 0.4 fusion.65
  18.8 0.4 fusion.68
  19.6 1.2 multiply_convert_fusion.2
  21.1 0.6 multiply_convert_fusion.1
  21.7 0.4 fusion.38
  22.2 0.4 fusion.39
  23.0 0.4 fusion.41
  23.5 0.4 fusion.42
  24.4 0.4 fusion.15
  24.8 1.6 fusion.7
  28.1 4.7 %collective-permute-start.5 = (bf16[1,64,1,384]{3,1,2,0:T(8,128)(2,1)S(1)}, bf16[1,64,1,384]{3,1,2,0:T(8,128)(2,1)S(1)}, u32[]{:S(2)}, u32[]{:S(2)}) collective-permute-start(bf16[1,64,1,384]{3,1,2,0:T(8,128)(2,1)S(1)} %get-tuple-element.15), channel_id=1, source_target_pairs={{1,0},{2,1},{3,2},{4,3},{5,4},{6,5},{7,6},{8,7},{9,8},{10,9},{11,1... | collective-permute-start | bytes 147464 | tf_op jit(solution)/shard_map/ppermute | solution.py:17
  32.9 5.4 %collective-permute-start.3 = (bf16[1,64,1,384]{3,1,2,0:T(8,128)(2,1)S(1)}, bf16[1,64,1,384]{3,1,2,0:T(8,128)(2,1)S(1)}, u32[]{:S(2)}, u32[]{:S(2)}) collective-permute-start(bf16[1,64,1,384]{3,1,2,0:T(8,128)(2,1)S(1)} %get-tuple-element.17), channel_id=1, source_target_pairs={{1,0},{2,1},{3,2},{4,3},{5,4},{6,5},{7,6},{8,7},{9,8},{10,9},{11,1... | collective-permute-start | bytes 147464 | tf_op jit(solution)/shard_map/ppermute | solution.py:17
  38.3 0.7 select_maximum_fusion
  39.0 0.5 convolution_bitcast_fusion.3
  39.9 0.4 convolution_bitcast_fusion.2
  40.3 0.7 convolution_bitcast_fusion
  41.0 0.4 convolution_bitcast_fusion.8
  41.5 0.7 convolution_bitcast_fusion.6
  42.2 0.9 multiply_convert_fusion
  43.1 0.7 convolution_bitcast_fusion.11
  43.8 0.7 convolution_bitcast_fusion.15
  44.5 0.7 convolution_bitcast_fusion.17
  45.2 0.7 convolution_bitcast_fusion.9
  45.9 1.6 fusion.29
  47.5 1.6 fusion.30
  49.1 1.6 fusion.31
  50.7 1.7 fusion.32
  52.4 1.6 fusion.33
  53.9 1.6 fusion.34
  55.5 1.7 fusion.35
  57.3 0.5 convolution_bitcast_fusion.1
  57.8 0.5 convolution_bitcast_fusion.7
  58.3 0.8 pad_maximum_fusion.6
  59.0 0.5 convolution_bitcast_fusion.10
  59.5 0.5 convolution_bitcast_fusion.16
  60.0 0.7 pad_maximum_fusion.5
  60.8 5.4 %fusion.8 = bf16[1,64,16,384]{3,1,2,0:T(8,128)(2,1)S(1)} fusion(f32[16,384,64]{1,2,0:T(8,128)} %fusion.29, f32[16,384,64]{1,2,0:T(8,128)} %fusion.30, f32[16,384,64]{1,2,0:T(8,128)} %fusion.31, f32[16,384,64]{1,2,0:T(8,128)S(1)} %fusion.47, f32[16,384,64]{1,2,0:T(8,128)} %fusion.32, f32[16,384,64]{1,2,0:T(8,128)} %fusion.33, f32[16,384,64]{1,2,0:T(8,128)} %fusion.35, ...), kind=kOutput, calls=%fused_computation.16 | convolution fusion | flops 54657024 | bytes 14958592 | tf_op jit(solution)/shard_map/oc,boij->bcij/dot_general | solution.py:64
  66.2 1.3 copy.38
  67.5 247.8 %all-reduce.8.cloned.1.call-done = (f32[3,3,64,64]{3,2,1,0:T(8,128)}, f32[3,3,64,64]{3,2,1,0:T(8,128)}) async-done(((f32[3,3,64,64]{3,2,1,0:T(8,128)}, f32[3,3,64,64]{3,2,1,0:T(8,128)}), (f32[3,3,64,64]{3,2,1,0:T(8,128)}, f32[3,3,64,64]{3,2,1,0:T(8,128)})) %all-reduce.8.cloned.1.call-update) | async-done | bytes 294928 | tf_op jit(solution)/shard_map/psum | solution.py:114
  315.2 1.7 multiply_convert_fusion.3
  316.9 1.7 multiply_convert_fusion.4
  (44 shorter events, 6.1 us)
Async XLA Ops:
  7.2 5.2 %copy-start.1 = (bf16[1,64,16,384]{3,2,1,0:T(8,128)(2,1)S(1)}, bf16[1,64,16,384]{3,2,1,0:T(8,128)(2,1)}, u32[]{:S(2)}) copy-start(bf16[1,64,16,384]{3,2,1,0:T(8,128)(2,1)} %param.5) | copy-start | bytes 2359300
  7.2 1.5 copy-start
  7.2 5.2 %copy-start.2 = (bf16[3,3,64,64]{3,2,1,0:T(8,128)(2,1)S(1)}, bf16[3,3,64,64]{3,2,1,0:T(8,128)(2,1)}, u32[]{:S(2)}) copy-start(bf16[3,3,64,64]{3,2,1,0:T(8,128)(2,1)} %param.7) | copy-start | bytes 221188
  7.2 308.1 %all-reduce.8.cloned.1.call-start = ((), (), s32[]{:S(2)}) async-start(), calls=%async_computation | async-start | bytes 1179648 | tf_op jit(solution)/shard_map/psum | solution.py:114
  8.9 3.8 %copy-start.4 = (bf16[3,3,64,64]{3,2,1,0:T(8,128)(2,1)S(1)}, bf16[3,3,64,64]{3,2,1,0:T(8,128)(2,1)}, u32[]{:S(2)}) copy-start(bf16[3,3,64,64]{3,2,1,0:T(8,128)(2,1)} %param.8) | copy-start | bytes 221188
  9.0 4.7 %collective-permute-start = (bf16[2,64,1,384]{3,1,2,0:T(8,128)(2,1)S(1)}, bf16[2,64,1,384]{3,1,2,0:T(8,128)(2,1)S(1)}, u32[]{:S(2)}, u32[]{:S(2)}) collective-permute-start(bf16[2,64,1,384]{3,1,2,0:T(8,128)(2,1)S(1)} %get-tuple-element.12), channel_id=1, source_target_pairs={{0,1},{1,2},{2,3},{3,4},{4,5},{5,6},{6,7},{7,8},{8,9},{9,10},{10,1... | collective-permute-start | bytes 294920 | tf_op jit(solution)/shard_map/ppermute | solution.py:16
  12.1 4.0 %collective-permute-start.1 = (bf16[2,64,1,384]{3,1,2,0:T(8,128)(2,1)S(1)}, bf16[2,64,1,384]{3,1,2,0:T(8,128)(2,1)S(1)}, u32[]{:S(2)}, u32[]{:S(2)}) collective-permute-start(bf16[2,64,1,384]{3,1,2,0:T(8,128)(2,1)S(1)} %get-tuple-element.13), channel_id=1, source_target_pairs={{1,0},{2,1},{3,2},{4,3},{5,4},{6,5},{7,6},{8,7},{9,8},{10,9},{11,1... | collective-permute-start | bytes 294920 | tf_op jit(solution)/shard_map/ppermute | solution.py:17
  12.7 0.7 copy-start.5
  28.0 10.3 %collective-permute-start.4 = (bf16[1,64,1,384]{3,1,2,0:T(8,128)(2,1)S(1)}, bf16[1,64,1,384]{3,1,2,0:T(8,128)(2,1)S(1)}, u32[]{:S(2)}, u32[]{:S(2)}) collective-permute-start(bf16[1,64,1,384]{3,1,2,0:T(8,128)(2,1)S(1)} %get-tuple-element.14), channel_id=1, source_target_pairs={{0,1},{1,2},{2,3},{3,4},{4,5},{5,6},{6,7},{7,8},{8,9},{9,10},{10,1... | collective-permute-start | bytes 147464 | tf_op jit(solution)/shard_map/ppermute | solution.py:16
  28.1 10.2 %collective-permute-start.5 = (bf16[1,64,1,384]{3,1,2,0:T(8,128)(2,1)S(1)}, bf16[1,64,1,384]{3,1,2,0:T(8,128)(2,1)S(1)}, u32[]{:S(2)}, u32[]{:S(2)}) collective-permute-start(bf16[1,64,1,384]{3,1,2,0:T(8,128)(2,1)S(1)} %get-tuple-element.15), channel_id=1, source_target_pairs={{1,0},{2,1},{3,2},{4,3},{5,4},{6,5},{7,6},{8,7},{9,8},{10,9},{11,1... | collective-permute-start | bytes 147464 | tf_op jit(solution)/shard_map/ppermute | solution.py:17
  32.9 9.3 %collective-permute-start.2 = (bf16[1,64,1,384]{3,1,2,0:T(8,128)(2,1)S(1)}, bf16[1,64,1,384]{3,1,2,0:T(8,128)(2,1)S(1)}, u32[]{:S(2)}, u32[]{:S(2)}) collective-permute-start(bf16[1,64,1,384]{3,1,2,0:T(8,128)(2,1)S(1)} %get-tuple-element.16), channel_id=1, source_target_pairs={{0,1},{1,2},{2,3},{3,4},{4,5},{5,6},{6,7},{7,8},{8,9},{9,10},{10,1... | collective-permute-start | bytes 147464 | tf_op jit(solution)/shard_map/ppermute | solution.py:16
  32.9 9.3 %collective-permute-start.3 = (bf16[1,64,1,384]{3,1,2,0:T(8,128)(2,1)S(1)}, bf16[1,64,1,384]{3,1,2,0:T(8,128)(2,1)S(1)}, u32[]{:S(2)}, u32[]{:S(2)}) collective-permute-start(bf16[1,64,1,384]{3,1,2,0:T(8,128)(2,1)S(1)} %get-tuple-element.17), channel_id=1, source_target_pairs={{1,0},{2,1},{3,2},{4,3},{5,4},{6,5},{7,6},{8,7},{9,8},{10,9},{11,1... | collective-permute-start | bytes 147464 | tf_op jit(solution)/shard_map/ppermute | solution.py:17
  44.5 1.4 copy-start.3
Sparse Core Ops, SparseCore 0:
  60.9 254.3 all-reduce.7
where the time goes:
time: 326 us; the launch traced here: 325 us
  waiting for transfers between devices  250 us (77%)
  matrix products  36 us (11%)
  between operations  14.5 us (4%)
  starting transfers between devices  13.7 us (4%)
  other arithmetic  7.25 us (2%)
  local copies, waits for them, and re-layouts  3.62 us (1%)
    psum x1, waiting for transfers between devices, per_device(): first, second = lax.psum((first, second), ('dp', 'lon'))  248 us
    dot_general x18, matrix products, stencil_adjoint(): jnp.einsum('oc,boij->bcij', taps[p, q], source[:, :, 2 - p:2 - p + column...  22.2 us
    ppermute x3, starting transfers between devices, extended(): after = lax.ppermute(first, axis, down)  10.4 us
    dot_general x18, matrix products, kernel_term(): jnp.einsum('boij,bcij->oc', source, padded[:, :, p:p + columns, q:q + lat...  9.32 us
  transfers between devices with their start and end apart: 7, of which 3 were waited for; matrix products, arithmetic and copies ran while one was open for 3% of the time, Pallas kernels for 0%

commit v1 on v0

--- a/solution.py
+++ b/solution.py
@@ -111,7 +111,8 @@
         cotangent.astype(jnp.float32) + stencil_adjoint(delta_pad, delta_scaled, kernel_first)
     ).astype(jnp.bfloat16)
     first = kernel_term(delta, delta_scaled[:, :, 1:-1, 1:-1], input_pad)
-    first, second = lax.psum((first, second), ("dp", "lon"))
+    switch_circles_on_mesh = lambda vals: lax.psum(lax.psum(vals, "dp"), "lon")
+    first, second = switch_circles_on_mesh((first, second))
     counted = (
         float(fields.shape[0] * lax.axis_size("dp"))
         * float(fields.shape[2] * lax.axis_size("lon"))

time: 326 us -> 411 us (1.26)
  waiting for transfers between devices: 250 us -> 333 us
    psum x1 -> x2, waiting for transfers between devices: 248 us -> 330 us  [per_device(): switch_circles_on_mesh = lambda vals: lax.psum(lax.psum(vals, 'dp'), 'lon')]
  transfers between devices with their start and end apart: 7 -> 8, of which waited for: 3 -> 4; matrix products, arithmetic and copies ran while one was open for 3% -> 4% of each run, Pallas kernels for 0% -> 0%
where the time goes in v1:
time: 411 us; the launch traced here: 410 us
  waiting for transfers between devices  333 us (81%)
  matrix products  37.4 us (9%)
  between operations  14.5 us (4%)
  starting transfers between devices  14.1 us (3%)
  other arithmetic  7.23 us (2%)
    psum x2, waiting for transfers between devices, per_device(): switch_circles_on_mesh = lambda vals: lax.psum(lax.psum(vals, 'dp'), 'lon')  330 us
    dot_general x18, matrix products, stencil_adjoint(): jnp.einsum('oc,boij->bcij', taps[p, q], source[:, :, 2 - p:2 - p + column...  23.6 us
    ppermute x3, starting transfers between devices, extended(): after = lax.ppermute(first, axis, down)  10.4 us
    dot_general x18, matrix products, kernel_term(): jnp.einsum('boij,bcij->oc', source, padded[:, :, p:p + columns, q:q + lat...  9.33 us
  transfers between devices with their start and end apart: 8, of which 4 were waited for; matrix products, arithmetic and copies ran while one was open for 4% of the time, Pallas kernels for 0%

profile of v1, /device:TPU:1, one launch (start us, length us, event | category | flops | bytes accessed | tf_op | source)
XLA Modules:
  0.0 409.8 jit_solution(15383977087420846891)
XLA Ops:
  7.2 1.4 copy_dynamic-update-slice_fusion
  9.0 3.1 collective-permute-start
  13.7 2.4 collective-permute-done.1
  16.6 0.4 fusion.53
  17.0 0.4 fusion.56
  17.5 0.4 fusion.59
  17.9 0.4 fusion.62
  18.3 0.4 fusion.65
  18.8 0.4 fusion.68
  19.6 1.2 multiply_convert_fusion.2
  21.1 0.6 multiply_convert_fusion.1
  21.7 0.4 fusion.38
  22.2 0.4 fusion.39
  23.0 0.4 fusion.41
  23.5 0.4 fusion.42
  24.8 1.6 fusion.7
  28.3 4.7 %collective-permute-start.5 = (bf16[1,64,1,384]{3,1,2,0:T(8,128)(2,1)S(1)}, bf16[1,64,1,384]{3,1,2,0:T(8,128)(2,1)S(1)}, u32[]{:S(2)}, u32[]{:S(2)}) collective-permute-start(bf16[1,64,1,384]{3,1,2,0:T(8,128)(2,1)S(1)} %get-tuple-element.17), channel_id=1, source_target_pairs={{1,0},{2,1},{3,2},{4,3},{5,4},{6,5},{7,6},{8,7},{9,8},{10,9},{11,1... | collective-permute-start | bytes 147464 | tf_op jit(solution)/shard_map/ppermute | solution.py:17
  33.1 5.4 %collective-permute-start.3 = (bf16[1,64,1,384]{3,1,2,0:T(8,128)(2,1)S(1)}, bf16[1,64,1,384]{3,1,2,0:T(8,128)(2,1)S(1)}, u32[]{:S(2)}, u32[]{:S(2)}) collective-permute-start(bf16[1,64,1,384]{3,1,2,0:T(8,128)(2,1)S(1)} %get-tuple-element.19), channel_id=1, source_target_pairs={{1,0},{2,1},{3,2},{4,3},{5,4},{6,5},{7,6},{8,7},{9,8},{10,9},{11,1... | collective-permute-start | bytes 147464 | tf_op jit(solution)/shard_map/ppermute | solution.py:17
  38.5 0.7 select_maximum_fusion
  39.2 0.5 convolution_bitcast_fusion.3
  40.1 0.4 convolution_bitcast_fusion.2
  40.5 0.7 convolution_bitcast_fusion
  41.2 0.4 convolution_bitcast_fusion.8
  41.7 0.7 convolution_bitcast_fusion.6
  42.4 0.9 multiply_convert_fusion
  43.3 0.7 convolution_bitcast_fusion.11
  44.0 0.7 convolution_bitcast_fusion.15
  44.7 0.7 convolution_bitcast_fusion.17
  45.3 0.7 convolution_bitcast_fusion.9
  46.0 1.6 fusion.29
  47.7 1.6 fusion.30
  49.3 1.6 fusion.31
  50.9 1.7 fusion.32
  52.5 1.5 fusion.33
  54.1 0.5 convolution_bitcast_fusion.1
  54.6 0.5 convolution_bitcast_fusion.7
  55.1 0.7 pad_maximum_fusion.6
  55.8 0.5 convolution_bitcast_fusion.10
  56.3 0.5 convolution_bitcast_fusion.16
  56.8 0.7 pad_maximum_fusion.5
  57.8 2.3 fusion.34
  60.2 2.4 fusion.35
  62.6 71.2 %all-reduce.12.cloned.1.call-done = (f32[3,3,64,64]{3,2,1,0:T(8,128)}, f32[3,3,64,64]{3,2,1,0:T(8,128)}) async-done(((f32[3,3,64,64]{3,2,1,0:T(8,128)}, f32[3,3,64,64]{3,2,1,0:T(8,128)}), (f32[3,3,64,64]{3,2,1,0:T(8,128)}, f32[3,3,64,64]{3,2,1,0:T(8,128)})) %all-reduce.12.cloned.1.call-update) | async-done | bytes 294928 | tf_op jit(solution)/shard_map/psum | solution.py:114
  133.9 5.4 %fusion.8 = bf16[1,64,16,384]{3,1,2,0:T(8,128)(2,1)S(1)} fusion(f32[16,384,64]{1,2,0:T(8,128)} %fusion.29, f32[16,384,64]{1,2,0:T(8,128)} %fusion.30, f32[16,384,64]{1,2,0:T(8,128)} %fusion.31, f32[16,384,64]{1,2,0:T(8,128)S(1)} %fusion.47, f32[16,384,64]{1,2,0:T(8,128)} %fusion.32, f32[16,384,64]{1,2,0:T(8,128)} %fusion.33, f32[16,384,64]{1,2,0:T(8,128)} %fusion.35, ...), kind=kOutput, calls=%fused_computation.16 | convolution fusion | flops 54657024 | bytes 14958592 | tf_op jit(solution)/shard_map/oc,boij->bcij/dot_general | solution.py:64
  139.2 1.3 copy.38
  140.6 259.0 %all-reduce.10.cloned.1.call-done = (f32[3,3,64,64]{3,2,1,0:T(8,128)}, f32[3,3,64,64]{3,2,1,0:T(8,128)}) async-done(((f32[3,3,64,64]{3,2,1,0:T(8,128)}, f32[3,3,64,64]{3,2,1,0:T(8,128)}), (f32[3,3,64,64]{3,2,1,0:T(8,128)}, f32[3,3,64,64]{3,2,1,0:T(8,128)})) %all-reduce.10.cloned.1.call-update) | async-done | bytes 294928 | tf_op jit(solution)/shard_map/psum | solution.py:114
  399.6 1.7 multiply_convert_fusion.3
  401.3 1.7 multiply_convert_fusion.4
  (47 shorter events, 7.0 us)
Async XLA Ops:
  7.2 5.2 %copy-start.1 = (bf16[1,64,16,384]{3,2,1,0:T(8,128)(2,1)S(1)}, bf16[1,64,16,384]{3,2,1,0:T(8,128)(2,1)}, u32[]{:S(2)}) copy-start(bf16[1,64,16,384]{3,2,1,0:T(8,128)(2,1)} %param.5) | copy-start | bytes 2359300
  7.2 1.5 copy-start
  7.2 5.2 %copy-start.2 = (bf16[3,3,64,64]{3,2,1,0:T(8,128)(2,1)S(1)}, bf16[3,3,64,64]{3,2,1,0:T(8,128)(2,1)}, u32[]{:S(2)}) copy-start(bf16[3,3,64,64]{3,2,1,0:T(8,128)(2,1)} %param.7) | copy-start | bytes 221188
  7.2 126.6 %all-reduce.12.cloned.1.call-start = ((), (), s32[]{:S(2)}) async-start(), calls=%async_computation.1 | async-start | bytes 1179648 | tf_op jit(solution)/shard_map/psum | solution.py:114
  8.9 3.8 copy-start.4
  9.0 4.7 %collective-permute-start = (bf16[2,64,1,384]{3,1,2,0:T(8,128)(2,1)S(1)}, bf16[2,64,1,384]{3,1,2,0:T(8,128)(2,1)S(1)}, u32[]{:S(2)}, u32[]{:S(2)}) collective-permute-start(bf16[2,64,1,384]{3,1,2,0:T(8,128)(2,1)S(1)} %get-tuple-element.14), channel_id=1, source_target_pairs={{0,1},{1,2},{2,3},{3,4},{4,5},{5,6},{6,7},{7,8},{8,9},{9,10},{10,1... | collective-permute-start | bytes 294920 | tf_op jit(solution)/shard_map/ppermute | solution.py:16
  12.1 4.0 collective-permute-start.1
  12.7 0.7 copy-start.5
  28.0 10.5 %collective-permute-start.4 = (bf16[1,64,1,384]{3,1,2,0:T(8,128)(2,1)S(1)}, bf16[1,64,1,384]{3,1,2,0:T(8,128)(2,1)S(1)}, u32[]{:S(2)}, u32[]{:S(2)}) collective-permute-start(bf16[1,64,1,384]{3,1,2,0:T(8,128)(2,1)S(1)} %get-tuple-element.16), channel_id=1, source_target_pairs={{0,1},{1,2},{2,3},{3,4},{4,5},{5,6},{6,7},{7,8},{8,9},{9,10},{10,1... | collective-permute-start | bytes 147464 | tf_op jit(solution)/shard_map/ppermute | solution.py:16
  28.3 10.2 %collective-permute-start.5 = (bf16[1,64,1,384]{3,1,2,0:T(8,128)(2,1)S(1)}, bf16[1,64,1,384]{3,1,2,0:T(8,128)(2,1)S(1)}, u32[]{:S(2)}, u32[]{:S(2)}) collective-permute-start(bf16[1,64,1,384]{3,1,2,0:T(8,128)(2,1)S(1)} %get-tuple-element.17), channel_id=1, source_target_pairs={{1,0},{2,1},{3,2},{4,3},{5,4},{6,5},{7,6},{8,7},{9,8},{10,9},{11,1... | collective-permute-start | bytes 147464 | tf_op jit(solution)/shard_map/ppermute | solution.py:17
  33.0 9.3 %collective-permute-start.2 = (bf16[1,64,1,384]{3,1,2,0:T(8,128)(2,1)S(1)}, bf16[1,64,1,384]{3,1,2,0:T(8,128)(2,1)S(1)}, u32[]{:S(2)}, u32[]{:S(2)}) collective-permute-start(bf16[1,64,1,384]{3,1,2,0:T(8,128)(2,1)S(1)} %get-tuple-element.18), channel_id=1, source_target_pairs={{0,1},{1,2},{2,3},{3,4},{4,5},{5,6},{6,7},{7,8},{8,9},{9,10},{10,1... | collective-permute-start | bytes 147464 | tf_op jit(solution)/shard_map/ppermute | solution.py:16
  33.1 9.3 %collective-permute-start.3 = (bf16[1,64,1,384]{3,1,2,0:T(8,128)(2,1)S(1)}, bf16[1,64,1,384]{3,1,2,0:T(8,128)(2,1)S(1)}, u32[]{:S(2)}, u32[]{:S(2)}) collective-permute-start(bf16[1,64,1,384]{3,1,2,0:T(8,128)(2,1)S(1)} %get-tuple-element.19), channel_id=1, source_target_pairs={{1,0},{2,1},{3,2},{4,3},{5,4},{6,5},{7,6},{8,7},{9,8},{10,9},{11,1... | collective-permute-start | bytes 147464 | tf_op jit(solution)/shard_map/ppermute | solution.py:17
  44.6 1.4 copy-start.3
  57.6 342.1 %all-reduce.10.cloned.1.call-start = ((), (), s32[]{:S(2)}) async-start(), calls=%async_computation | async-start | bytes 1179648 | tf_op jit(solution)/shard_map/psum | solution.py:114
Sparse Core Ops, SparseCore 0:
  57.7 76.1 all-reduce.11
  136.5 263.0 all-reduce.9
